TPU v7x, 512 devices: a whole 4x4x16 slice. The times are simulated.
512 devices in a mesh: rows: 32 (over y_lo, z), filt: 16 (over y_hi, x, core).
Axes of the slice: x: 4, y: 4 (y_hi: 2, y_lo: 2; y = y_hi * 2 + y_lo), z: 16, core: 2. Of those that a mesh axis runs over, the one named last changes fastest.
Arguments:
- features: bfloat16 [512, 32, 512], P('filt', 'rows'), may hold values from -6 to 6
- first_weight: bfloat16 [512, 3, 3, 512], P('filt'), may hold values from -0.09375 to 0.09375
- second_weight: bfloat16 [512, 3, 3, 512], P('filt'), may hold values from -0.09375 to 0.09375
- out_grad: bfloat16 [512, 32, 512], P('filt', 'rows'), may hold values from -0.046875 to 0.046875
Outputs:
- block_out: bfloat16 [512, 32, 512], P('filt', 'rows')
- first_grad: float32 [512, 3, 3, 512], P('filt')
- second_grad: float32 [512, 3, 3, 512], P('filt')
All inputs are finite; a program needn't handle non-finite values.
Results may differ from a plain program's by a relative error of at most 0.024.
The roundings to bfloat16 on the way count: a program that leaves them out, or rounds other values in their place, can miss the bound.
Values may be sent and summed in bfloat16 or wider, within the bound.
A program may use at most 64 MiB of HBM per device.

v0:
```python
import jax
import jax.numpy as jnp
from jax import lax
from jax.sharding import PartitionSpec as P


def extended(cells, sides, width):
    for axis, dim in sides:
        count = lax.axis_size(axis)
        ends = count - 1
        head = lax.slice_in_dim(cells, 0, width, axis=dim)
        tail = lax.slice_in_dim(cells, cells.shape[dim] - width, cells.shape[dim], axis=dim)
        cells = jnp.concatenate(
            [
                lax.ppermute(tail, axis, [(i, (i + 1) % count) for i in range(ends)]),
                cells,
                lax.ppermute(head, axis, [((i + 1) % count, i) for i in range(ends)]),
            ],
            axis=dim,
        )
    return cells


def shift_cols(value, offset):
    if offset == 0:
        return value
    if offset > 0:
        return jnp.pad(value[..., offset:], ((0, 0), (0, 0), (0, offset)))
    return jnp.pad(value[..., :offset], ((0, 0), (0, 0), (-offset, 0)))


def conv_forward(weight, padded, count):
    total = jnp.zeros((weight.shape[0], count, padded.shape[2]), jnp.float32)
    for a in range(3):
        for b in range(3):
            part = jnp.einsum(
                "oi,ihw->ohw",
                weight[:, a, b, :],
                padded[:, a : a + count, :],
                preferred_element_type=jnp.float32,
            )
            total = total + shift_cols(part, b - 1)
    return total


def conv_backward(weight, padded, count):
    total = jnp.zeros((weight.shape[3], count, padded.shape[2]), jnp.float32)
    for a in range(3):
        for b in range(3):
            part = jnp.einsum(
                "oi,ohw->ihw",
                weight[:, a, b, :],
                padded[:, 2 - a : 2 - a + count, :],
                preferred_element_type=jnp.float32,
            )
            total = total + shift_cols(part, 1 - b)
    return total


def weight_terms(grad, padded, count):
    rows_out = []
    for a in range(3):
        cols_out = []
        for b in range(3):
            moved = shift_cols(grad, 1 - b)
            cols_out.append(
                jnp.einsum(
                    "ohw,ihw->oi",
                    moved,
                    padded[:, a : a + count, :],
                    preferred_element_type=jnp.float32,
                )
            )
        rows_out.append(jnp.stack(cols_out, axis=1))
    return jnp.stack(rows_out, axis=1)


def with_rims(value):
    return extended(value, (("rows", 1),), 1)


def all_channels(value):
    return lax.all_gather(with_rims(value), "filt", axis=0, tiled=True)


def per_device(features, first_weight, second_weight, out_grad):
    count = features.shape[1]
    padded_in = all_channels(features)
    pre_first = conv_forward(first_weight, padded_in, count)
    hidden = jnp.maximum(pre_first, 0.0).astype(jnp.bfloat16)
    padded_hidden = all_channels(hidden)
    pre_second = conv_forward(second_weight, padded_hidden, count) + features.astype(jnp.float32)
    block_out = jnp.maximum(pre_second, 0.0).astype(jnp.bfloat16)
    grad_second = jnp.where(pre_second > 0, out_grad.astype(jnp.float32), 0.0).astype(jnp.bfloat16)
    rimmed_grad = with_rims(grad_second)
    terms = conv_backward(second_weight, rimmed_grad, count)
    hidden_grad = lax.psum_scatter(terms, "filt", scatter_dimension=0, tiled=True)
    grad_first = jnp.where(pre_first > 0, hidden_grad, 0.0).astype(jnp.bfloat16)
    second_local = weight_terms(grad_second, padded_hidden, count)
    first_local = weight_terms(grad_first, padded_in, count)
    first_grad, second_grad = lax.psum((first_local, second_local), "rows")
    return (block_out, first_grad, second_grad)


def solution(mesh):
    in_specs = (
        P("filt", "rows", None),
        P("filt", None, None, None),
        P("filt", None, None, None),
        P("filt", "rows", None),
    )
    out_specs = (P("filt", "rows", None), P("filt", None, None, None), P("filt", None, None, None))
    return jax.shard_map(
        per_device, mesh=mesh, in_specs=in_specs, out_specs=out_specs, check_vma=False
    )
```

profile of v0, /device:TPU:2, one launch (start us, length us, event | category | flops | bytes accessed | tf_op | source)
XLA Modules:
  0.0 543.7 jit_solution(2598938622587336115)
XLA Ops:
  7.2 4.0 collective-permute-start
  11.2 1.3 collective-permute-start.1
  12.5 0.6 collective-permute-done
  13.1 4.1 collective-permute-done.1
  17.2 1.4 pad_maximum_fusion.2
  18.7 66.2 %all-gather.3.cloned.1.call-done = bf16[512,3,512]{2,0,1:T(8,128)(2,1)} async-done(((bf16[32,3,512]{2,0,1:T(8,128)(2,1)}), bf16[512,3,512]{2,0,1:T(8,128)(2,1)}) %all-gather.3.cloned.1.call-update) | async-done | bytes 1572880 | tf_op jit(solution)/shard_map/all_gather | solution.py:83
  84.9 1.4 convolution_bitcast_fusion.24
  86.4 1.3 convolution_bitcast_fusion.21
  87.7 1.2 convolution_bitcast_fusion.18
  89.5 0.2 convolution_bitcast_fusion.20
  89.7 0.2 fusion.9
  90.1 0.8 maximum_convert_fusion.1
  90.9 3.4 collective-permute-start.2
  94.4 1.3 collective-permute-start.3
  95.7 0.3 collective-permute-done.2
  96.0 4.2 collective-permute-done.3
  100.2 0.7 pad_maximum_fusion.3
  100.9 61.3 %all-gather.5.cloned.1.call-done = bf16[512,3,512]{2,0,1:T(8,128)(2,1)} async-done(((bf16[32,3,512]{2,0,1:T(8,128)(2,1)}), bf16[512,3,512]{2,0,1:T(8,128)(2,1)}) %all-gather.5.cloned.1.call-update) | async-done | bytes 1572880 | tf_op jit(solution)/shard_map/all_gather | solution.py:83
  162.2 1.3 convolution_bitcast_fusion.15
  163.7 1.2 convolution_bitcast_fusion.12
  165.0 1.2 convolution_bitcast_fusion.9
  166.5 0.2 convolution_bitcast_fusion.17
  166.9 0.2 fusion.14
  167.2 0.2 fusion.16
  167.4 0.8 maximum_convert_fusion
  168.3 1.3 collective-permute-start.4
  169.6 4.5 collective-permute-start.5
  174.1 0.3 convolution_bitcast_fusion.5
  174.5 0.3 convolution_bitcast_fusion.3
  174.8 0.3 convolution_bitcast_fusion.4
  175.2 0.3 slice.251
  175.5 0.3 convolution_bitcast_fusion.8
  175.9 0.3 slice.249
  176.2 0.3 convolution_bitcast_fusion.2
  176.6 0.3 slice.253
  176.9 0.3 convolution_bitcast_fusion
  177.2 0.3 convolution_bitcast_fusion.6
  177.6 0.3 convolution_bitcast_fusion.7
  177.9 2.0 fusion.1
  180.0 0.2 convolution_bitcast_fusion.27
  180.3 0.3 convolution_bitcast_fusion.29
  180.5 0.3 convolution_bitcast_fusion.28
  180.8 0.2 convolution_bitcast_fusion.30
  181.1 0.3 convolution_bitcast_fusion.32
  181.4 0.3 convolution_bitcast_fusion.33
  181.6 0.3 convolution_bitcast_fusion.35
  181.9 0.3 convolution_bitcast_fusion.31
  182.2 0.3 convolution_bitcast_fusion.34
  182.5 0.9 pad_maximum_fusion.1
  183.4 87.0 %reduce-scatter.2.cloned.1.call-done = f32[32,1,512]{2,0,1:T(8,128)} async-done(((f32[512,1,512]{2,0,1:T(8,128)}), f32[32,1,512]{2,0,1:T(8,128)}) %reduce-scatter.2.cloned.1.call-update) | async-done | bytes 65552 | tf_op jit(solution)/shard_map/reduce_scatter | solution.py:97
  270.4 0.8 select_convert_fusion
  271.3 0.2 convolution_bitcast_fusion.37
  271.6 0.3 convolution_bitcast_fusion.38
  271.8 0.3 convolution_bitcast_fusion.36
  272.1 0.2 convolution_bitcast_fusion.39
  272.4 0.3 convolution_bitcast_fusion.41
  272.7 0.3 convolution_bitcast_fusion.42
  272.9 0.3 convolution_bitcast_fusion.44
  273.2 0.3 convolution_bitcast_fusion.40
  273.5 0.3 convolution_bitcast_fusion.43
  273.8 0.9 pad_maximum_fusion
  274.7 259.7 %all-reduce.25.cloned.1.call-done = (f32[32,3,3,512]{3,0,2,1:T(8,128)}, f32[32,3,3,512]{3,0,2,1:T(8,128)}) async-done(((f32[32,3,3,512]{3,0,2,1:T(8,128)}, f32[32,3,3,512]{3,0,2,1:T(8,128)}), (f32[32,3,3,512]{3,0,2,1:T(8,128)}, f32[32,3,3,512]{3,0,2,1:T(8,128)})) %all-reduce.25.cloned.1.call-update) | async-done | bytes 1179664 | tf_op jit(solution)/shard_map/psum | solution.py:101
  534.3 2.0 copy.27
  536.3 0.8 copy.28
  (44 shorter events, 2.1 us)
Async XLA Ops:
  7.2 80.6 %copy-start.4 = (bf16[32,3,3,512]{3,0,2,1:T(8,128)(2,1)S(1)}, bf16[32,3,3,512]{3,0,2,1:T(8,128)(2,1)}, u32[]{:S(2)}) copy-start(bf16[32,3,3,512]{3,0,2,1:T(8,128)(2,1)} %param.5) | copy-start | bytes 884740
  7.2 77.8 %all-gather.3.cloned.1.call-start = ((), (), s32[]{:S(2)}) async-start(), calls=%async_computation.1 | async-start | bytes 1671168 | tf_op jit(solution)/shard_map/all_gather | solution.py:83
  7.2 5.9 %collective-permute-start = (bf16[32,1,512]{2,0,1:T(8,128)(2,1)}, bf16[32,1,512]{2,0,1:T(8,128)(2,1)S(1)}, u32[]{:S(2)}, u32[]{:S(2)}) collective-permute-start(bf16[32,1,512]{2,0,1:T(8,128)(2,1)} %param.4), channel_id=1, source_target_pairs={{0,16},{16,32},{32,48},{48,64},{64,80},{80,96},{96,112},{112,128},... | collective-permute-start | bytes 98312 | tf_op jit(solution)/shard_map/ppermute | solution.py:15
  11.2 6.0 %collective-permute-start.1 = (bf16[32,1,512]{2,0,1:T(8,128)(2,1)}, bf16[32,1,512]{2,0,1:T(8,128)(2,1)S(1)}, u32[]{:S(2)}, u32[]{:S(2)}) collective-permute-start(bf16[32,1,512]{2,0,1:T(8,128)(2,1)} %param.4), channel_id=1, source_target_pairs={{16,0},{32,16},{48,32},{64,48},{80,64},{96,80},{112,96},{128,112},... | collective-permute-start | bytes 98312 | tf_op jit(solution)/shard_map/ppermute | solution.py:17
  18.6 143.6 %all-gather.5.cloned.1.call-start = ((), (), s32[]{:S(2)}) async-start(), calls=%async_computation.2 | async-start | bytes 1671168 | tf_op jit(solution)/shard_map/all_gather | solution.py:83
  84.9 4.1 copy-start
  89.5 72.8 %copy-start.2 = (bf16[32,3,3,512]{3,0,2,1:T(8,128)(2,1)S(1)}, bf16[32,3,3,512]{3,0,2,1:T(8,128)(2,1)}, u32[]{:S(2)}) copy-start(bf16[32,3,3,512]{3,0,2,1:T(8,128)(2,1)} %param.6) | copy-start | bytes 884740
  90.9 5.0 collective-permute-start.2
  94.4 5.8 %collective-permute-start.3 = (bf16[32,1,512]{2,0,1:T(8,128)(2,1)S(1)}, bf16[32,1,512]{2,0,1:T(8,128)(2,1)S(1)}, u32[]{:S(2)}, u32[]{:S(2)}) collective-permute-start(bf16[32,1,512]{2,0,1:T(8,128)(2,1)S(1)} %get-tuple-element.9), channel_id=1, source_target_pairs={{16,0},{32,16},{48,32},{64,48},{80,64},{96,80},{112,96},{128,112},... | collective-permute-start | bytes 98312 | tf_op jit(solution)/shard_map/ppermute | solution.py:17
  100.9 169.5 %reduce-scatter.2.cloned.1.call-start = ((), (), s32[]{:S(2)}) async-start(), calls=%async_computation.3 | async-start | bytes 1114112 | tf_op jit(solution)/shard_map/reduce_scatter | solution.py:97
  162.2 4.1 copy-start.1
  166.5 0.8 copy-start.6
  166.7 1.5 copy-start.7
  168.3 7.2 %collective-permute-start.4 = (bf16[32,1,512]{2,0,1:T(8,128)(2,1)S(1)}, bf16[32,1,512]{2,0,1:T(8,128)(2,1)S(1)}, u32[]{:S(2)}, u32[]{:S(2)}) collective-permute-start(bf16[32,1,512]{2,0,1:T(8,128)(2,1)S(1)} %select_convert_fusion.1), channel_id=1, source_target_pairs={{16,0},{32,16},{48,32},{64,48},{80,64},{96,80},{112,96},{128,112},... | collective-permute-start | bytes 98312 | tf_op jit(solution)/shard_map/ppermute | solution.py:17
  169.6 6.6 %collective-permute-start.5 = (bf16[32,1,512]{2,0,1:T(8,128)(2,1)S(1)}, bf16[32,1,512]{2,0,1:T(8,128)(2,1)S(1)}, u32[]{:S(2)}, u32[]{:S(2)}) collective-permute-start(bf16[32,1,512]{2,0,1:T(8,128)(2,1)S(1)} %select_convert_fusion.1), channel_id=1, source_target_pairs={{0,16},{16,32},{32,48},{48,64},{64,80},{80,96},{96,112},{112,128},... | collective-permute-start | bytes 98312 | tf_op jit(solution)/shard_map/ppermute | solution.py:15
  180.0 354.4 %all-reduce.25.cloned.1.call-start = ((), (), s32[]{:S(2)}) async-start(), calls=%async_computation.4 | async-start | bytes 2359296 | tf_op jit(solution)/shard_map/psum | solution.py:101
  181.9 88.5 %copy-start.5 = (f32[32,1,512]{2,0,1:T(8,128)S(1)}, f32[32,1,512]{2,0,1:T(8,128)}, u32[]{:S(2)}) copy-start(f32[32,1,512]{2,0,1:T(8,128)} %get-tuple-element.10) | copy-start | bytes 196612
  534.3 2.0 copy-start.3
Sparse Core Ops, SparseCore 0:
  18.8 66.1 all-gather.2
  101.0 61.2 all-gather.4
  180.1 90.2 reduce-scatter.1
  274.8 259.5 all-reduce.24
where the time goes:
time: 544 us
  waiting for transfers between devices  484 us (89%)
  matrix products  20.8 us (4%)
  starting transfers between devices  16 us (3%)
  between operations  14 us (3%)
    psum x1, waiting for transfers between devices, per_device(): first_grad, second_grad = lax.psum((first_local, second_local), 'rows')  260 us
    all_gather x2, waiting for transfers between devices, all_channels(): return lax.all_gather(with_rims(value), 'filt', axis=0, tiled=True)  128 us
    reduce_scatter x1, waiting for transfers between devices, per_device(): lax.psum_scatter(terms, 'filt', scatter_dimension=0, tiled=True)  87 us
    ppermute x3, starting transfers between devices, extended(): lax.ppermute(tail, axis, [(i, (i + 1) % count) for i in range(ends)])  12 us
    dot_general x18, matrix products, conv_forward(): jnp.einsum('oi,ihw->ohw', weight[:, a, b, :], padded[:, a:a + count, :],...  11.3 us
  transfers between devices with their start and end apart: 10, of which 8 were waited for; matrix products, arithmetic and copies ran while one was open for 1% of the time, Pallas kernels for 0%

commit v1 on v0

--- a/solution.py
+++ b/solution.py
@@ -2,6 +2,13 @@
 import jax.numpy as jnp
 from jax import lax
 from jax.sharding import PartitionSpec as P
+
+
+def exchange_gather(x, mesh_axis, dim):
+    size = lax.axis_size(mesh_axis)
+    shards = jnp.stack([x for _ in range(size)])
+    shards = lax.all_to_all(shards, mesh_axis, split_axis=0, concat_axis=0)
+    return jnp.concatenate(shards, axis=dim)
 
 
 def extended(cells, sides, width):
@@ -80,7 +87,7 @@
 
 
 def all_channels(value):
-    return lax.all_gather(with_rims(value), "filt", axis=0, tiled=True)
+    return exchange_gather(with_rims(value), "filt", 0)
 
 
 def per_device(features, first_weight, second_weight, out_grad):

time: 544 us -> 469 us (0.86)
  waiting for transfers between devices: 484 us -> 360 us
  blocking collectives: 0 us -> 53.2 us
  matrix products: 20.8 us -> 13.7 us
    all_gather x2 -> x0, waiting for transfers between devices: 128 us -> none  [all_channels(): return lax.all_gather(with_rims(value), 'filt', axis=0, tiled=True)]
    all_to_all x0 -> x2, blocking collectives: none -> 53.2 us  [exchange_gather(): shards = lax.all_to_all(shards, mesh_axis, split_axis=0, concat_axis=0)]
    dot_general x18, matrix products: 11.3 us -> 4.2 us  [conv_forward(): jnp.einsum('oi,ihw->ohw', weight[:, a, b, :], padded[:, a:a + count, :],...]
  transfers between devices with their start and end apart: 10 -> 8, of which waited for: 8 -> 6; matrix products, arithmetic and copies ran while one was open for 1% -> 1% of each run, Pallas kernels for 0% -> 0%
where the time goes in v1:
time: 469 us
  waiting for transfers between devices  360 us (77%)
  blocking collectives  53.2 us (11%)
  starting transfers between devices  17.4 us (4%)
  between operations  14.3 us (3%)
  matrix products  13.7 us (3%)
  local copies, waits for them, and re-layouts  6.76 us (1%)
    psum x1, waiting for transfers between devices, per_device(): first_grad, second_grad = lax.psum((first_local, second_local), 'rows')  259 us
    reduce_scatter x1, waiting for transfers between devices, per_device(): lax.psum_scatter(terms, 'filt', scatter_dimension=0, tiled=True)  90 us
    all_to_all x2, blocking collectives, exchange_gather(): shards = lax.all_to_all(shards, mesh_axis, split_axis=0, concat_axis=0)  53.2 us
    ppermute x3, starting transfers between devices, extended(): lax.ppermute(tail, axis, [(i, (i + 1) % count) for i in range(ends)])  13.4 us
    ppermute x3, waiting for transfers between devices, extended(): lax.ppermute(head, axis, [((i + 1) % count, i) for i in range(ends)])  9.51 us
  transfers between devices with their start and end apart: 8, of which 6 were waited for; matrix products, arithmetic and copies ran while one was open for 1% of the time, Pallas kernels for 0%

profile of v1, /device:TPU:2, one launch (start us, length us, event | category | flops | bytes accessed | tf_op | source)
XLA Modules:
  0.0 468.6 jit_solution(13412460129985256843)
XLA Ops:
  7.2 3.8 collective-permute-start
  11.0 1.3 collective-permute-start.1
  12.3 0.6 collective-permute-done
  12.9 4.1 collective-permute-done.1
  17.1 0.8 pad_maximum_fusion.2
  18.0 27.2 %all_to_all.10 = bf16[16,32,3,512]{3,1,2,0:T(8,128)(2,1)S(1)} all-to-all(bf16[16,32,3,512]{3,1,2,0:T(8,128)(2,1)S(1)} %stack.134), channel_id=1, replica_groups=mesh['rows'=32,'filt'=16] {'filt'}, dimensions={0} | all-to-all | bytes 3145728 | tf_op jit(solution)/shard_map/all_to_all | solution.py:10
  45.4 0.9 copy-done.2
  46.4 0.2 convolution_bitcast_fusion.23
  46.6 0.2 convolution_bitcast_fusion.26
  46.8 0.2 convolution_bitcast_fusion.21
  47.0 0.2 convolution_bitcast_fusion.20
  47.2 0.2 convolution_bitcast_fusion.18
  47.7 0.2 fusion.9
  47.9 0.2 fusion.11
  48.1 0.2 maximum_convert_fusion.1
  48.3 3.8 collective-permute-start.2
  52.1 1.3 collective-permute-start.3
  53.4 0.5 collective-permute-done.2
  53.9 5.4 %collective-permute-done.3 = bf16[32,1,512]{2,0,1:T(8,128)(2,1)S(1)} collective-permute-done((bf16[32,1,512]{2,0,1:T(8,128)(2,1)S(1)}, bf16[32,1,512]{2,0,1:T(8,128)(2,1)S(1)}, u32[]{:S(2)}, u32[]{:S(2)}) %collective-permute-start.3) | collective-permute-done | bytes 32800 | tf_op jit(solution)/shard_map/ppermute | solution.py:24
  59.5 25.9 %all_to_all.11 = bf16[16,32,3,512]{3,1,2,0:T(8,128)(2,1)S(1)} all-to-all(bf16[16,32,3,512]{3,1,2,0:T(8,128)(2,1)S(1)} %stack.135), channel_id=1, replica_groups=mesh['rows'=32,'filt'=16] {'filt'}, dimensions={0} | all-to-all | bytes 3145728 | tf_op jit(solution)/shard_map/all_to_all | solution.py:10
  85.5 0.9 copy-done
  86.6 0.2 convolution_bitcast_fusion.14
  86.8 0.2 convolution_bitcast_fusion.17
  87.8 0.2 fusion.14
  88.3 0.8 maximum_convert_fusion
  89.2 1.3 collective-permute-start.4
  90.5 5.8 %collective-permute-start.5 = (bf16[32,1,512]{2,0,1:T(8,128)(2,1)S(1)}, bf16[32,1,512]{2,0,1:T(8,128)(2,1)S(1)}, u32[]{:S(2)}, u32[]{:S(2)}) collective-permute-start(bf16[32,1,512]{2,0,1:T(8,128)(2,1)S(1)} %select_convert_fusion.1), channel_id=1, source_target_pairs={{0,16},{16,32},{32,48},{48,64},{64,80},{80,96},{96,112},{112,128},... | collective-permute-start | bytes 98312 | tf_op jit(solution)/shard_map/ppermute | solution.py:22
  96.2 0.3 convolution_bitcast_fusion.5
  96.6 0.3 convolution_bitcast_fusion.3
  96.9 0.3 convolution_bitcast_fusion.4
  97.3 0.3 slice.251
  97.6 0.3 convolution_bitcast_fusion.8
  98.0 0.3 slice.249
  98.3 0.3 convolution_bitcast_fusion.2
  98.6 0.3 slice.253
  99.0 0.3 convolution_bitcast_fusion
  99.3 0.3 convolution_bitcast_fusion.6
  99.7 0.3 convolution_bitcast_fusion.7
  100.0 2.0 fusion.1
  102.1 0.2 convolution_bitcast_fusion.27
  102.3 0.3 convolution_bitcast_fusion.29
  102.6 0.3 convolution_bitcast_fusion.28
  102.9 0.2 convolution_bitcast_fusion.30
  103.1 0.3 convolution_bitcast_fusion.32
  103.4 0.3 convolution_bitcast_fusion.33
  103.7 0.3 convolution_bitcast_fusion.35
  104.0 0.3 convolution_bitcast_fusion.31
  104.2 0.3 convolution_bitcast_fusion.34
  104.6 0.9 pad_maximum_fusion.1
  105.4 90.0 %reduce-scatter.2.cloned.1.call-done = f32[32,1,512]{2,0,1:T(8,128)} async-done(((f32[512,1,512]{2,0,1:T(8,128)}), f32[32,1,512]{2,0,1:T(8,128)}) %reduce-scatter.2.cloned.1.call-update) | async-done | bytes 65552 | tf_op jit(solution)/shard_map/reduce_scatter | solution.py:104
  195.4 0.8 select_convert_fusion
  196.3 0.2 convolution_bitcast_fusion.40
  196.6 0.3 convolution_bitcast_fusion.41
  196.8 0.3 convolution_bitcast_fusion.44
  197.1 0.3 convolution_bitcast_fusion.43
  197.4 0.3 convolution_bitcast_fusion.39
  197.6 0.3 convolution_bitcast_fusion.42
  197.9 0.3 convolution_bitcast_fusion.38
  198.2 0.3 convolution_bitcast_fusion.37
  198.4 0.3 convolution_bitcast_fusion.36
  198.8 0.9 pad_maximum_fusion
  199.7 259.3 %all-reduce.25.cloned.1.call-done = (f32[32,3,3,512]{3,0,2,1:T(8,128)}, f32[32,3,3,512]{3,0,2,1:T(8,128)}) async-done(((f32[32,3,3,512]{3,0,2,1:T(8,128)}, f32[32,3,3,512]{3,0,2,1:T(8,128)}), (f32[32,3,3,512]{3,0,2,1:T(8,128)}, f32[32,3,3,512]{3,0,2,1:T(8,128)})) %all-reduce.25.cloned.1.call-update) | async-done | bytes 1179664 | tf_op jit(solution)/shard_map/psum | solution.py:108
  459.0 2.0 copy.49
  461.0 0.8 copy.50
  (38 shorter events, 2.7 us)
Async XLA Ops:
  7.2 188.2 %reduce-scatter.2.cloned.1.call-start = ((), (), s32[]{:S(2)}) async-start(), calls=%async_computation.3 | async-start | bytes 1114112 | tf_op jit(solution)/shard_map/reduce_scatter | solution.py:104
  7.2 5.7 %collective-permute-start = (bf16[32,1,512]{2,0,1:T(8,128)(2,1)}, bf16[32,1,512]{2,0,1:T(8,128)(2,1)S(1)}, u32[]{:S(2)}, u32[]{:S(2)}) collective-permute-start(bf16[32,1,512]{2,0,1:T(8,128)(2,1)} %param.4), channel_id=1, source_target_pairs={{0,16},{16,32},{32,48},{48,64},{64,80},{80,96},{96,112},{112,128},... | collective-permute-start | bytes 98312 | tf_op jit(solution)/shard_map/ppermute | solution.py:22
  11.0 6.0 %collective-permute-start.1 = (bf16[32,1,512]{2,0,1:T(8,128)(2,1)}, bf16[32,1,512]{2,0,1:T(8,128)(2,1)S(1)}, u32[]{:S(2)}, u32[]{:S(2)}) collective-permute-start(bf16[32,1,512]{2,0,1:T(8,128)(2,1)} %param.4), channel_id=1, source_target_pairs={{16,0},{32,16},{48,32},{64,48},{80,64},{96,80},{112,96},{128,112},... | collective-permute-start | bytes 98312 | tf_op jit(solution)/shard_map/ppermute | solution.py:24
  45.3 1.0 copy-start.2
  48.3 5.6 %collective-permute-start.2 = (bf16[32,1,512]{2,0,1:T(8,128)(2,1)S(1)}, bf16[32,1,512]{2,0,1:T(8,128)(2,1)S(1)}, u32[]{:S(2)}, u32[]{:S(2)}) collective-permute-start(bf16[32,1,512]{2,0,1:T(8,128)(2,1)S(1)} %get-tuple-element.9), channel_id=1, source_target_pairs={{0,16},{16,32},{32,48},{48,64},{64,80},{80,96},{96,112},{112,128},... | collective-permute-start | bytes 98312 | tf_op jit(solution)/shard_map/ppermute | solution.py:22
  52.1 7.1 %collective-permute-start.3 = (bf16[32,1,512]{2,0,1:T(8,128)(2,1)S(1)}, bf16[32,1,512]{2,0,1:T(8,128)(2,1)S(1)}, u32[]{:S(2)}, u32[]{:S(2)}) collective-permute-start(bf16[32,1,512]{2,0,1:T(8,128)(2,1)S(1)} %get-tuple-element.9), channel_id=1, source_target_pairs={{16,0},{32,16},{48,32},{64,48},{80,64},{96,80},{112,96},{128,112},... | collective-permute-start | bytes 98312 | tf_op jit(solution)/shard_map/ppermute | solution.py:24
  85.4 1.0 copy-start
  87.2 1.1 copy-start.3
  87.6 1.5 copy-start.4
  89.2 8.4 %collective-permute-start.4 = (bf16[32,1,512]{2,0,1:T(8,128)(2,1)S(1)}, bf16[32,1,512]{2,0,1:T(8,128)(2,1)S(1)}, u32[]{:S(2)}, u32[]{:S(2)}) collective-permute-start(bf16[32,1,512]{2,0,1:T(8,128)(2,1)S(1)} %select_convert_fusion.1), channel_id=1, source_target_pairs={{16,0},{32,16},{48,32},{64,48},{80,64},{96,80},{112,96},{128,112},... | collective-permute-start | bytes 98312 | tf_op jit(solution)/shard_map/ppermute | solution.py:24
  90.5 7.8 %collective-permute-start.5 = (bf16[32,1,512]{2,0,1:T(8,128)(2,1)S(1)}, bf16[32,1,512]{2,0,1:T(8,128)(2,1)S(1)}, u32[]{:S(2)}, u32[]{:S(2)}) collective-permute-start(bf16[32,1,512]{2,0,1:T(8,128)(2,1)S(1)} %select_convert_fusion.1), channel_id=1, source_target_pairs={{0,16},{16,32},{32,48},{48,64},{64,80},{80,96},{96,112},{112,128},... | collective-permute-start | bytes 98312 | tf_op jit(solution)/shard_map/ppermute | solution.py:22
  102.0 356.9 %all-reduce.25.cloned.1.call-start = ((), (), s32[]{:S(2)}) async-start(), calls=%async_computation.4 | async-start | bytes 2359296 | tf_op jit(solution)/shard_map/psum | solution.py:108
  459.0 2.0 copy-start.1
Sparse Core Ops, SparseCore 0:
  102.2 93.1 reduce-scatter.1
  199.8 259.1 all-reduce.24
